TPU v7x, 32 devices: a whole 2x2x4 slice. The times are simulated.
32 devices in a mesh: groups: 2 (over y), band: 4 (over z), img: 2 (over x), col: 2 (over core).
Axes of the slice: x: 2, y: 2, z: 4, core: 2. Of those that a mesh axis runs over, the one named last changes fastest.
Arguments:
- real_images: float32 [4, 64, 3, 128], P(('groups', 'img'), ('band', 'col')), parts along dimension 0, may hold values from -6 to 6
- tile_images: float32 [4, 64, 3, 128], P(('groups', 'img'), 'band', None, 'col'), parts along dimension 0, may hold values from -6 to 6
- rgb_weight: float32 [3, 64], replicated, may hold values from -3.5 to 3.5
- first_weight: float32 [3, 3, 64, 64], replicated, may hold values from -0.25 to 0.25
- second_weight: float32 [3, 3, 64, 128], replicated, may hold values from -0.25 to 0.25
- skip_weight: float32 [64, 128], replicated, may hold values from -0.75 to 0.75
- readout: float32 [32, 128, 64], P(('band', 'col')), may hold values from -0.01171875 to 0.01171875
Outputs:
- grad_rgb: float32 [6, 64], P('groups'), parts along dimension 0
- grad_first: float32 [6, 3, 64, 64], P('groups'), parts along dimension 0
- grad_second: float32 [6, 3, 64, 128], P('groups'), parts along dimension 0
- grad_skip: float32 [128, 128], P('groups'), parts along dimension 0
There are 2 independent parts, one for each index of `groups`. A program takes and returns all parts, laid end to end along the dimension named above; an argument that names none is the same for every part. Nothing has to cross between parts.
All inputs are finite; a program needn't handle non-finite values.
Results may differ from a plain program's by a relative error of at most 0.00019.
Values sent between devices are 32-bit elements; how exact they have to be, the bound alone decides.
A program may use at most 64 MiB of HBM per device.

v0:
```python
import functools

import jax
import jax.numpy as jnp
from jax import lax
from jax.experimental import pallas as pl
from jax.experimental.pallas import tpu as pltpu
from jax.sharding import PartitionSpec as P

INV_ROOT = 0.7071067811865476
GAMMA_WEIGHT = 10.0
F32 = jnp.float32
BF16 = jnp.bfloat16


def halves(x):
    hi = x.astype(BF16)
    return hi, (x - hi.astype(F32)).astype(BF16)


def dot_nn(a, b):
    return lax.dot_general(a, b, (((1,), (0,)), ((), ())), preferred_element_type=F32)


def dot_nt(a, b):
    return lax.dot_general(a, b, (((1,), (1,)), ((), ())), preferred_element_type=F32)


def sigmoid(u):
    return 0.5 + 0.5 * jnp.tanh(0.5 * u)


def step_kernel(
    rows, vr, vf, ro, mask, rgbt, wf, wt, w2, sk, out,
    wfs, wts, w2s, us_h, us_l, uz_h, uz_l, zs, gh,
    fr, fr_h, fr_l, sp, s2, gp_h, gp_l, psp, ps2, hs, gf,
    df_h, df_l, ff_h, ff_l, fsp, ap_h, ap_l, gq_h, gq_l, as_h, as_l, fs, hx_h, hx_l, du,
):
    feat, wide, cols = rgbt.shape[0], ro.shape[1], vr.shape[2]
    half = cols // 2
    first, last = 4, 4 + rows

    def at(w, count=1):
        return slice(w * cols, (w + count) * cols)

    lane = lax.broadcasted_iota(jnp.int32, (feat, cols), 1)

    def right(x):
        return jnp.where(lane == 0, 0.0, pltpu.roll(x, 1, 1))

    def left(x):
        return jnp.where(lane == cols - 1, 0.0, pltpu.roll(x, cols - 1, 1))

    def split_weights(ref, dst, base, count):
        hi, lo = halves(ref[...])
        dst[base : base + ref.shape[0]] = hi
        dst[count + base : count + base + ref.shape[0]] = lo

    split_weights(wf, wfs, 0, 3 * feat)
    split_weights(wt, wts, 0, 3 * feat)
    split_weights(w2, w2s, 0, 10 * feat)
    split_weights(sk, w2s, 9 * feat, 10 * feat)

    def product(weights, count, x_hi, x_lo):
        full = weights[...]
        both = dot_nn(full, x_hi)
        return both[:count] + both[count:] + dot_nn(full[:count], x_lo)

    pick_row = lax.broadcasted_iota(jnp.int32, (half, cols), 0)
    pick_col = lax.broadcasted_iota(jnp.int32, (half, cols), 1)
    picks = [(pick_col == 2 * pick_row + (j - 1)).astype(F32).astype(BF16) for j in range(3)]
    out_rows = rows // 2
    for t in range(out_rows + 4):
        hi, lo = halves(ro[t] * INV_ROOT)
        uz_h[:, at(t)] = dot_nn(hi, picks[1]).astype(BF16)
        uz_l[:, at(t)] = dot_nn(lo, picks[1]).astype(BF16)
        if 2 <= t < 2 + out_rows:
            for j in range(3):
                us_h[j * wide : (j + 1) * wide, at(t - 2)] = dot_nn(hi, picks[j]).astype(BF16)
                us_l[j * wide : (j + 1) * wide, at(t - 2)] = dot_nn(lo, picks[j]).astype(BF16)
    for t in range(0, out_rows + 4, 2):
        zs[:, at(t, 2)] = product(w2s, 10 * feat, uz_h[:, at(t, 2)], uz_l[:, at(t, 2)])

    def tap(i, j, t):
        base = (i * 3 + j) * feat
        return zs[base : base + feat, at(t)]

    for w in range(1, last + 3):
        if w % 2 == 0:
            parts = [tap(1, j, w // 2) for j in range(3)]
        else:
            parts = [tap(2, j, (w - 1) // 2) + tap(0, j, (w + 1) // 2) for j in range(3)]
        value = parts[1] + left(parts[0]) + right(parts[2])
        gh[:, at(w)] = value * mask[w : w + 1, :]

    rgb = [rgbt[:, c : c + 1] for c in range(3)]

    def project(rows3):
        return rgb[0] * rows3[0:1, :] + rgb[1] * rows3[1:2, :] + rgb[2] * rows3[2:3, :]

    def put(hi_ref, lo_ref, w, value):
        hi, lo = halves(value)
        hi_ref[:, at(w)] = hi
        lo_ref[:, at(w)] = lo

    for w in range(last + 4):
        u = project(vr[w])
        s = sigmoid(u)
        value = u * s
        put(fr_h, fr_l, w, value)
        if first <= w < last and w % 2 == 0:
            fs[:, at((w - first) // 2)] = -value
        sp[:, at(w)] = s * (1.0 + u * (1.0 - s))
        s2[:, at(w)] = s * (1.0 - s) * (2.0 + u * (1.0 - 2.0 * s))
    for w in range(2, last + 2):
        u = project(vf[w - 2])
        s = sigmoid(u)
        value = u * s
        put(ff_h, ff_l, w, value)
        if first <= w < last and w % 2 == 0:
            fs[:, at((w - first) // 2)] += value
        fsp[:, at(w)] = s * (1.0 + u * (1.0 - s))

    def convolve(weights, hi_ref, lo_ref, w):
        x_hi = jnp.concatenate([hi_ref[:, at(w + k, 2)] for k in (-1, 0, 1)], 0)
        x_lo = jnp.concatenate([lo_ref[:, at(w + k, 2)] for k in (-1, 0, 1)], 0)
        y = product(weights, 3 * feat, x_hi, x_lo)
        return [
            (w + k, [y[j * feat : (j + 1) * feat, at(k)] for j in range(3)]) for k in range(2)
        ]

    def forward(hi_ref, lo_ref, w):
        for row, y in convolve(wfs, hi_ref, lo_ref, w):
            yield row, y[1] + right(y[0]) + left(y[2])

    def backward(hi_ref, lo_ref, w):
        for row, y in convolve(wts, hi_ref, lo_ref, w):
            yield row, y[1] + left(y[0]) + right(y[2])

    span = rows * cols

    def put_shifts(field, w, value):
        lanes = slice(field * span + (w - first) * cols, field * span + (w - first + 1) * cols)
        for j, moved in enumerate((left(value), value, right(value))):
            hi, lo = halves(moved)
            as_h[j * feat : (j + 1) * feat, lanes] = hi
            as_l[j * feat : (j + 1) * feat, lanes] = lo

    for start in range(1, last + 3, 2):
        for w, u in forward(fr_h, fr_l, start):
            s = sigmoid(u)
            prime = s * (1.0 + u * (1.0 - s))
            grad = gh[:, at(w)] * prime
            put(gp_h, gp_l, w, grad)
            if first <= w < last:
                put_shifts(2, w, GAMMA_WEIGHT * grad)
            if 3 <= w <= last:
                psp[:, at(w)] = prime
                ps2[:, at(w)] = s * (1.0 - s) * (2.0 + u * (1.0 - 2.0 * s))
                hs[:, at(w)] = -(u * s) * mask[w : w + 1, :]

    for start in range(3, last + 1, 2):
        for w, u in forward(ff_h, ff_l, start):
            s = sigmoid(u)
            grad = gh[:, at(w)] * (s * (1.0 + u * (1.0 - s)))
            put(gq_h, gq_l, w, grad)
            if first <= w < last:
                put_shifts(1, w, grad)
            hs[:, at(w)] += u * s * mask[w : w + 1, :]

    def add_skip(w, value):
        if w % 2 == 0:
            return value + zs[9 * feat : 10 * feat, at(w // 2)]
        return value

    zero = jnp.zeros((feat, cols), F32)
    acc = [zero, zero, zero]
    for start in range(2, last + 2, 2):
        for w, y in backward(gp_h, gp_l, start):
            value = add_skip(w, y)
            gu = value * sp[:, at(w)]
            keep = mask[w : w + 1, :]
            g = [jnp.sum(rgb[c] * gu, axis=0, keepdims=True) * keep for c in range(3)]
            moved = rgb[0] * g[0] + rgb[1] * g[1] + rgb[2] * g[2]
            tangent = sp[:, at(w)] * moved
            put(df_h, df_l, w, tangent)
            if first <= w < last:
                if w % 2 == 0:
                    fs[:, at((w - first) // 2)] += GAMMA_WEIGHT * tangent
                gf[:, at(w)] = GAMMA_WEIGHT * value * moved * s2[:, at(w)]
                acc = [acc[c] + (GAMMA_WEIGHT * g[c]) * gu for c in range(3)]

    for start in range(first, last, 2):
        for w, y in backward(gq_h, gq_l, start):
            gu = add_skip(w, y) * fsp[:, at(w)]
            image = vf[w - 2]
            acc = [acc[c] + image[c : c + 1, :] * gu for c in range(3)]

    for start in range(3, last + 1, 2):
        for w, dp in forward(df_h, df_l, start):
            hidden_grad = gh[:, at(w)]
            prime = psp[:, at(w)]
            total = hidden_grad * (GAMMA_WEIGHT * ps2[:, at(w)] * dp - prime)
            put(ap_h, ap_l, w, total)
            if first <= w < last:
                put_shifts(0, w, total)
            hs[:, at(w)] += GAMMA_WEIGHT * prime * dp * mask[w : w + 1, :]

    for start in range(first, last, 2):
        for w, y in backward(ap_h, ap_l, start):
            if w % 2 == 0:
                y = y - zs[9 * feat : 10 * feat, at(w // 2)]
            au = y * sp[:, at(w)] + gf[:, at(w)]
            image = vr[w]
            acc = [acc[c] + image[c : c + 1, :] * au for c in range(3)]

    for r in range(out_rows):
        for i in range(3):
            hi, lo = halves(hs[:, at(3 + 2 * r + i)])
            hx_h[i * feat : (i + 1) * feat, at(r)] = hi
            hx_l[i * feat : (i + 1) * feat, at(r)] = lo
        hi, lo = halves(fs[:, at(r)])
        hx_h[3 * feat : 4 * feat, at(r)] = hi
        hx_l[3 * feat : 4 * feat, at(r)] = lo
    second = (
        dot_nt(hx_h[...], us_h[...])
        + dot_nt(hx_l[...], us_h[...])
        + dot_nt(hx_h[...], us_l[...])
    )
    for i in range(3):
        for j in range(3):
            base = (i * 3 + j) * feat
            out[base : base + feat, :] = second[
                i * feat : (i + 1) * feat, j * wide : (j + 1) * wide
            ]
    out[9 * feat : 10 * feat, :] = second[3 * feat : 4 * feat, wide : 2 * wide]

    grad = None
    for field, (hi_ref, lo_ref) in enumerate(((fr_h, fr_l), (ff_h, ff_l), (df_h, df_l))):
        lanes = slice(field * span, (field + 1) * span)
        x_hi = jnp.concatenate([hi_ref[:, at(3 + i, rows)] for i in range(3)], 0)
        x_lo = jnp.concatenate([lo_ref[:, at(3 + i, rows)] for i in range(3)], 0)
        a_hi, a_lo = as_h[:, lanes], as_l[:, lanes]
        term = dot_nt(x_hi, a_hi) + dot_nt(x_lo, a_hi) + dot_nt(x_hi, a_lo)
        grad = term if grad is None else grad + term
    base = 10 * feat
    out[base : base + 3 * feat, :] = grad[:, : 2 * feat]
    tail = grad[:, 2 * feat :]
    base = 13 * feat
    out[base : base + feat, :] = jnp.concatenate([tail[:feat], tail[feat : 2 * feat]], 1)
    spot = lax.broadcasted_iota(jnp.int32, (feat, feat), 1)
    colour = jnp.zeros((feat, feat), F32)
    for c in range(3):
        colour = jnp.where(spot == c, jnp.sum(acc[c], axis=1, keepdims=True), colour)
    base = 14 * feat
    out[base : base + feat, :] = jnp.concatenate([tail[2 * feat :], colour], 1)


def local_step(vr, vf, ro, mask, rgb_weight, first_weight, second_weight, skip_weight):
    rows = vr.shape[0] - 8
    feat, wide = skip_weight.shape
    cols = vr.shape[2]
    wf = jnp.transpose(first_weight, (1, 3, 0, 2)).reshape(3 * feat, 3 * feat)
    wt = jnp.transpose(first_weight[::-1], (1, 2, 0, 3)).reshape(3 * feat, 3 * feat)
    w2 = second_weight.reshape(9 * feat, wide)

    def keep(height, count, kind):
        return pltpu.VMEM((height, count * cols), kind)

    def pair(height, count):
        return [keep(height, count, BF16), keep(height, count, BF16)]

    window, outs = rows + 8, rows // 2
    plain = keep(feat, window, F32)
    scratch = [
        pltpu.VMEM((6 * feat, 3 * feat), BF16),
        pltpu.VMEM((6 * feat, 3 * feat), BF16),
        pltpu.VMEM((20 * feat, wide), BF16),
        *pair(3 * wide, outs),
        *pair(wide, outs + 4),
        keep(10 * feat, outs + 4, F32),
        plain,
        plain, *pair(feat, window), plain, plain,
        *pair(feat, window), plain, plain, plain, plain,
        *pair(feat, window),
        *pair(feat, window), plain,
        *pair(feat, window), *pair(feat, window),
        *pair(3 * feat, 3 * rows),
        keep(feat, outs, F32), *pair(4 * feat, outs), plain,
    ]
    whole = pl.BlockSpec(memory_space=pltpu.VMEM)
    return pl.pallas_call(
        functools.partial(step_kernel, rows),
        out_shape=jax.ShapeDtypeStruct((15 * feat, wide), F32),
        in_specs=[whole] * 9,
        out_specs=whole,
        scratch_shapes=scratch,
        compiler_params=pltpu.CompilerParams(vmem_limit_bytes=60 * 1024 * 1024),
    )(vr, vf, ro, mask, rgb_weight.T, wf, wt, w2, skip_weight)


def neighbours(cells, above, below):
    axes = ("band", "col")
    count = lax.axis_size(axes)
    links = count - 1
    down = [(i, i + 1) for i in range(links)]
    up = [(i + 1, i) for i in range(links)]
    before = lax.ppermute(cells[cells.shape[0] - above :], axes, down)
    after = lax.ppermute(cells[:below], axes, up)
    return jnp.concatenate([before, cells, after], 0)


def unpack(total, feat):
    second = total[: 9 * feat].reshape(3, 3, feat, total.shape[1])
    skip = total[9 * feat : 10 * feat]
    pairs = total[10 * feat : 13 * feat].reshape(3, feat, 2, feat)
    low = total[13 * feat : 14 * feat]
    high = total[14 * feat : 15 * feat]
    third = jnp.stack([low[:, :feat], low[:, feat:], high[:, :feat]])
    grad_first = jnp.stack([pairs[:, :, 0], pairs[:, :, 1], third], 1)
    return high[:, feat : feat + 3].T, grad_first, second, skip


def body(real_images, tile_images, rgb_weight, first_weight, second_weight, skip_weight, readout):
    row_count = real_images.shape[1]
    axes = ("band", "col")
    total_rows = row_count * lax.axis_size(axes)
    generated = lax.all_to_all(tile_images, "col", split_axis=1, concat_axis=3, tiled=True)
    vr = neighbours(real_images[0], 4, 4)
    vf = neighbours(generated[0], 2, 2)
    ro = neighbours(readout, 2, 2)
    rows = lax.axis_index(axes) * row_count - 4 + jnp.arange(row_count + 8)
    inside = ((rows >= 0) & (rows < total_rows)).astype(F32)
    mask = jnp.broadcast_to(inside[:, None], (row_count + 8, real_images.shape[3]))
    packed = local_step(vr, vf, ro, mask, rgb_weight, first_weight, second_weight, skip_weight)
    return unpack(lax.psum(packed, ("band", "img", "col")), skip_weight.shape[0])


def solution(mesh):
    placed = (
        P(("groups", "img"), ("band", "col"), None, None),
        P(("groups", "img"), "band", None, "col"),
        P(),
        P(),
        P(),
        P(),
        P(("band", "col"), None, None),
    )
    return jax.shard_map(
        body,
        mesh=mesh,
        in_specs=placed,
        out_specs=(
            P("groups", None),
            P("groups", None, None, None),
            P("groups", None, None, None),
            P("groups", None),
        ),
        check_vma=False,
    )
```

profile of v0, /device:TPU:0, one launch (start us, length us, event | category | flops | bytes accessed | tf_op | source)
XLA Modules:
  0.0 153.4 jit_solution(12908801833436307421)
XLA Ops:
  7.2 0.0 all-reduce.2.cloned.1.call-start
  7.2 0.7 copy.65
  7.9 0.0 copy-start.3
  7.9 2.4 %collective-permute-start = (f32[4,3,128]{2,1,0:T(4,128)S(1)}, f32[4,3,128]{2,1,0:T(4,128)S(1)}, u32[]{:S(2)}, u32[]{:S(2)}) collective-permute-start(f32[4,3,128]{2,1,0:T(4,128)S(1)} %get-tuple-element.25), channel_id=1, source_target_pairs={{0,1},{1,4},{4,5},{5,8},{8,9},{9,12},{12,13},{2,3},{3,6},{6,7},{7,... | collective-permute-start | bytes 18440 | tf_op jit(solution)/shard_map/ppermute | solution.py:308
  10.3 1.3 collective-permute-start.1
  11.6 0.0 copy-done.3
  11.7 0.0 copy-start.2
  11.7 0.1 reshape.41
  11.8 6.5 %all_to_all.15 = f32[2,1,1536]{2,1,0:T(1,128)S(1)} all-to-all(f32[2,1,1536]{2,1,0:T(1,128)S(1)} %reshape.41), channel_id=1, replica_groups=mesh['groups'=2,'band'=4,'img'=2,'col'=2] {'col'}, dimensions={0} | all-to-all | bytes 24576 | tf_op jit(solution)/shard_map/all_to_all | solution.py:328
  18.3 0.5 broadcast.22
  18.8 0.7 reduce
  19.5 0.1 reshape.42
  19.6 0.1 slice.70
  19.7 1.3 collective-permute-start.3
  21.0 0.1 slice.68
  21.1 3.0 %collective-permute-start.2 = (f32[2,3,128]{2,1,0:T(4,128)S(1)}, f32[2,3,128]{2,1,0:T(4,128)S(1)}, u32[]{:S(2)}, u32[]{:S(2)}) collective-permute-start(f32[2,3,128]{2,1,0:T(4,128)S(1)} %copy.45), channel_id=1, source_target_pairs={{0,1},{1,4},{4,5},{5,8},{8,9},{9,12},{12,13},{2,3},{3,6},{6,7},{7,... | collective-permute-start | bytes 9224 | tf_op jit(solution)/shard_map/ppermute | solution.py:308
  24.1 0.0 copy-done.2
  24.1 0.1 copy.48
  24.3 0.0 copy-start
  24.3 3.8 %collective-permute-start.4 = (f32[2,128,64]{2,1,0:T(8,128)S(1)}, f32[2,128,64]{2,1,0:T(8,128)S(1)}, u32[]{:S(2)}, u32[]{:S(2)}) collective-permute-start(f32[2,128,64]{2,1,0:T(8,128)S(1)} %get-tuple-element.19), channel_id=1, source_target_pairs={{0,1},{1,4},{4,5},{5,8},{8,9},{9,12},{12,13},{2,3},{3,6},{6,7},{7,... | collective-permute-start | bytes 196616 | tf_op jit(solution)/shard_map/ppermute | solution.py:308
  28.1 0.0 copy-done
  28.2 0.1 squeeze.7
  28.3 0.0 copy-start.4
  28.3 0.7 copy-done.4
  28.9 0.7 copy.51
  29.6 0.2 copy.53
  29.8 0.9 reshape.37.wt
  30.8 0.2 copy.52
  31.0 0.9 reshape.36.wf
  31.9 0.0 collective-permute-done.3
  31.9 1.3 collective-permute-start.5
  33.2 0.0 collective-permute-done.2
  33.2 0.6 pad_maximum_fusion.3.vf
  33.8 0.0 collective-permute-done
  33.8 0.0 collective-permute-done.1
  33.8 0.6 pad_maximum_fusion.2.vr
  34.4 0.0 collective-permute-done.4
  34.5 0.7 collective-permute-done.5
  35.1 0.8 pad_maximum_fusion.ro
  36.0 0.7 broadcast_in_dim.2.mask
  36.6 9.6 %shard_map.102 = f32[960,128]{1,0:T(8,128)} custom-call(f32[16,3,128]{2,1,0:T(4,128)} %pad_maximum_fusion.2.vr, f32[12,3,128]{2,1,0:T(4,128)} %pad_maximum_fusion.3.vf, f32[8,128,64]{2,1,0:T(8,128)} %pad_maximum_fusion.ro, f32[16,128]{1,0:T(8,128)} %broadcast_in_dim.2.mask, f32[64,3]{1,0:T(8,128)} %bitcast.51, f32[192,192]{1,0:T(8,128)} %reshape.36.wf, ...), custom_call_target="tpu_custom_call" | custom-call | tf_op jit(solution)/shard_map/pallas_call | solution.py:292
  46.3 0.0 all-reduce.2.cloned.1.call-update
  46.3 95.3 %all-reduce.2.cloned.1.call-done = f32[960,128]{1,0:T(8,128)} async-done(((f32[960,128]{1,0:T(8,128)}), f32[960,128]{1,0:T(8,128)}) %all-reduce.2.cloned.1.call-update) | async-done | bytes 491536 | tf_op jit(solution)/shard_map/psum | solution.py:336
  141.6 0.8 slice_bitcast_fusion.3
  142.4 0.7 copy.56
  143.1 0.0 slice-start
  143.1 0.0 copy-start.1
  143.1 0.9 slice-done
  144.0 0.2 reshape.39
  144.2 0.2 fusion.1
  144.3 0.0 copy-done.1
  144.3 0.1 slice_bitcast_fusion.2
  144.4 0.7 copy.57
  145.2 0.6 slice.96
  145.8 0.7 slice.95
  (12 shorter events, 0.1 us)
Async XLA Ops:
  7.2 134.4 %all-reduce.2.cloned.1.call-start = ((), (), s32[]{:S(2)}) async-start(), calls=%async_computation.1 | async-start | bytes 983040 | tf_op jit(solution)/shard_map/psum | solution.py:336
  7.9 3.7 %copy-start.3 = (f32[1,16,3,64]{3,1,2,0:T(8,128)S(1)}, f32[1,16,3,64]{3,1,2,0:T(8,128)}, u32[]{:S(2)}) copy-start(f32[1,16,3,64]{3,1,2,0:T(8,128)} %param.8) | copy-start | bytes 36868
  7.9 25.9 %collective-permute-start = (f32[4,3,128]{2,1,0:T(4,128)S(1)}, f32[4,3,128]{2,1,0:T(4,128)S(1)}, u32[]{:S(2)}, u32[]{:S(2)}) collective-permute-start(f32[4,3,128]{2,1,0:T(4,128)S(1)} %get-tuple-element.25), channel_id=1, source_target_pairs={{0,1},{1,4},{4,5},{5,8},{8,9},{9,12},{12,13},{2,3},{3,6},{6,7},{7,... | collective-permute-start | bytes 18440 | tf_op jit(solution)/shard_map/ppermute | solution.py:308
  10.3 23.5 %collective-permute-start.1 = (f32[4,3,128]{2,1,0:T(4,128)S(1)}, f32[4,3,128]{2,1,0:T(4,128)S(1)}, u32[]{:S(2)}, u32[]{:S(2)}) collective-permute-start(f32[4,3,128]{2,1,0:T(4,128)S(1)} %get-tuple-element.26), channel_id=1, source_target_pairs={{1,0},{4,1},{5,4},{8,5},{9,8},{12,9},{13,12},{3,2},{6,3},{7,6},{10... | collective-permute-start | bytes 18440 | tf_op jit(solution)/shard_map/ppermute | solution.py:309
  11.7 12.5 %copy-start.2 = (f32[4,128,64]{1,2,0:T(8,128)S(1)}, f32[4,128,64]{1,2,0:T(8,128)}, u32[]{:S(2)}) copy-start(f32[4,128,64]{1,2,0:T(8,128)} %param.13) | copy-start | bytes 393220
  19.7 12.2 %collective-permute-start.3 = (f32[2,3,128]{2,1,0:T(4,128)S(1)}, f32[2,3,128]{2,1,0:T(4,128)S(1)}, u32[]{:S(2)}, u32[]{:S(2)}) collective-permute-start(f32[2,3,128]{2,1,0:T(4,128)S(1)} %copy.46), channel_id=1, source_target_pairs={{1,0},{4,1},{5,4},{8,5},{9,8},{12,9},{13,12},{3,2},{6,3},{7,6},{10... | collective-permute-start | bytes 9224 | tf_op jit(solution)/shard_map/ppermute | solution.py:309
  21.1 12.1 %collective-permute-start.2 = (f32[2,3,128]{2,1,0:T(4,128)S(1)}, f32[2,3,128]{2,1,0:T(4,128)S(1)}, u32[]{:S(2)}, u32[]{:S(2)}) collective-permute-start(f32[2,3,128]{2,1,0:T(4,128)S(1)} %copy.45), channel_id=1, source_target_pairs={{0,1},{1,4},{4,5},{5,8},{8,9},{9,12},{12,13},{2,3},{3,6},{6,7},{7,... | collective-permute-start | bytes 9224 | tf_op jit(solution)/shard_map/ppermute | solution.py:308
  24.3 3.8 %copy-start = (f32[3,3,64,64]{3,2,1,0:T(8,128)S(1)}, f32[3,3,64,64]{3,2,1,0:T(8,128)}, u32[]{:S(2)}) copy-start(f32[3,3,64,64]{3,2,1,0:T(8,128)} %param.10) | copy-start | bytes 442372
  24.3 10.1 %collective-permute-start.4 = (f32[2,128,64]{2,1,0:T(8,128)S(1)}, f32[2,128,64]{2,1,0:T(8,128)S(1)}, u32[]{:S(2)}, u32[]{:S(2)}) collective-permute-start(f32[2,128,64]{2,1,0:T(8,128)S(1)} %get-tuple-element.19), channel_id=1, source_target_pairs={{0,1},{1,4},{4,5},{5,8},{8,9},{9,12},{12,13},{2,3},{3,6},{6,7},{7,... | collective-permute-start | bytes 196616 | tf_op jit(solution)/shard_map/ppermute | solution.py:308
  28.3 0.7 copy-start.4
  31.9 3.2 %collective-permute-start.5 = (f32[2,128,64]{2,1,0:T(8,128)S(1)}, f32[2,128,64]{2,1,0:T(8,128)S(1)}, u32[]{:S(2)}, u32[]{:S(2)}) collective-permute-start(f32[2,128,64]{2,1,0:T(8,128)S(1)} %get-tuple-element.20), channel_id=1, source_target_pairs={{1,0},{4,1},{5,4},{8,5},{9,8},{12,9},{13,12},{3,2},{6,3},{7,6},{10... | collective-permute-start | bytes 196616 | tf_op jit(solution)/shard_map/ppermute | solution.py:309
  143.1 0.9 slice-start
  143.1 1.2 copy-start.1
Sparse Core Ops, SparseCore 0:
  46.4 95.1 all-reduce.1
where the time goes:
time: 154 us; the launch traced here: 153 us
  waiting for transfers between devices  96 us (62%)
  between operations  14.3 us (9%)
  starting transfers between devices  13.1 us (9%)
  local copies, waits for them, and re-layouts  11.1 us (7%)
  Pallas kernels  9.64 us (6%)
  blocking collectives  6.52 us (4%)
  other arithmetic  2.79 us (2%)
    psum x1, waiting for transfers between devices, body(): lax.psum(packed, ('band', 'img', 'col'))  95.3 us
    pallas_call x1, Pallas kernels, local_step(): pl.pallas_call(functools.partial(step_kernel, rows), out_shape=jax.ShapeD...  9.64 us
    ppermute x3, starting transfers between devices, neighbours(): before = lax.ppermute(cells[cells.shape[0] - above:], axes, down)  9.2 us
    all_to_all x1, blocking collectives, body(): lax.all_to_all(tile_images, 'col', split_axis=1, concat_axis=3, tiled=True)  6.52 us
    ppermute x3, starting transfers between devices, neighbours(): after = lax.ppermute(cells[:below], axes, up)  3.85 us
    unnamed x18, local copies, waits for them, and re-layouts  3.83 us
  transfers between devices with their start and end apart: 7, of which 2 were waited for; matrix products, arithmetic and copies ran while one was open for 4% of the time, Pallas kernels for 0%

commit v1 on v0

--- a/solution.py
+++ b/solution.py
@@ -254,6 +254,104 @@
         colour = jnp.where(spot == c, jnp.sum(acc[c], axis=1, keepdims=True), colour)
     base = 14 * feat
     out[base : base + feat, :] = jnp.concatenate([tail[2 * feat :], colour], 1)
+    if out.shape[0] > 15 * feat:
+        out[15 * feat :, :] = jnp.zeros((out.shape[0] - 15 * feat, wide), F32)
+
+
+REDUCE_AXES = ("col", "img", "band")
+
+
+def reduce_kernel(sizes, x, out, *scratch):
+    count = len(sizes)
+    arrive, sums = scratch[:count], scratch[count : 2 * count - 1]
+    send_in, recv_in = scratch[2 * count - 1 : 3 * count - 1], scratch[3 * count - 1 : 4 * count - 1]
+    send_out, recv_out = scratch[4 * count - 1 : 5 * count - 1], scratch[5 * count - 1 :]
+    places = [lax.axis_index(name) for name in REDUCE_AXES]
+
+    barrier = pltpu.get_barrier_semaphore()
+    for k, name in enumerate(REDUCE_AXES):
+        for d in range(1, sizes[k]):
+            pl.semaphore_signal(
+                barrier,
+                inc=1,
+                device_id={name: lax.rem(places[k] + d, sizes[k])},
+                device_id_type=pl.DeviceIdType.MESH,
+            )
+    pl.semaphore_wait(barrier, sum(sizes) - count)
+
+    held, offset, height = x, 0, x.shape[0]
+    spans = []
+    for k, name in enumerate(REDUCE_AXES):
+        spans.append((offset, height))
+        height = height // sizes[k]
+        copies = []
+        for d in range(1, sizes[k]):
+            peer = lax.rem(places[k] + d, sizes[k])
+            copies.append(
+                pltpu.make_async_remote_copy(
+                    src_ref=held.at[pl.ds(pl.multiple_of(peer * height, 8), height)],
+                    dst_ref=arrive[k].at[d - 1],
+                    send_sem=send_in[k].at[d - 1],
+                    recv_sem=recv_in[k].at[d - 1],
+                    device_id={name: peer},
+                    device_id_type=pl.DeviceIdType.MESH,
+                )
+            )
+        for copy in copies:
+            copy.start()
+        for copy in copies:
+            copy.wait()
+        total = held[pl.ds(pl.multiple_of(places[k] * height, 8), height), :]
+        for d in range(1, sizes[k]):
+            total = total + arrive[k][d - 1]
+        offset = offset + places[k] * height
+        if k < count - 1:
+            sums[k][...] = total
+            held = sums[k]
+        else:
+            out[pl.ds(pl.multiple_of(offset, 8), height), :] = total
+
+    for k in reversed(range(count)):
+        name = REDUCE_AXES[k]
+        height = spans[k][1] // sizes[k]
+        own = pl.ds(pl.multiple_of(spans[k][0] + places[k] * height, 8), height)
+        copies = []
+        for d in range(1, sizes[k]):
+            copies.append(
+                pltpu.make_async_remote_copy(
+                    src_ref=out.at[own],
+                    dst_ref=out.at[own],
+                    send_sem=send_out[k].at[d - 1],
+                    recv_sem=recv_out[k].at[d - 1],
+                    device_id={name: lax.rem(places[k] + d, sizes[k])},
+                    device_id_type=pl.DeviceIdType.MESH,
+                )
+            )
+        for copy in copies:
+            copy.start()
+        for copy in copies:
+            copy.wait()
+
+
+def reduce_all(packed):
+    sizes = [lax.axis_size(name) for name in REDUCE_AXES]
+    height, width = packed.shape
+    arrive, sums = [], []
+    for k, size in enumerate(sizes):
+        height = height // size
+        arrive.append(pltpu.VMEM((size - 1, height, width), F32))
+        if k < len(sizes) - 1:
+            sums.append(pltpu.VMEM((height, width), F32))
+    waits = [pltpu.SemaphoreType.DMA((size - 1,)) for size in sizes]
+    whole = pl.BlockSpec(memory_space=pltpu.VMEM)
+    return pl.pallas_call(
+        functools.partial(reduce_kernel, sizes),
+        out_shape=jax.ShapeDtypeStruct(packed.shape, F32),
+        in_specs=[whole],
+        out_specs=whole,
+        scratch_shapes=[*arrive, *sums, *waits, *waits, *waits, *waits],
+        compiler_params=pltpu.CompilerParams(collective_id=0, has_side_effects=True),
+    )(packed)
 
 
 def local_step(vr, vf, ro, mask, rgb_weight, first_weight, second_weight, skip_weight):
@@ -289,9 +387,10 @@
         keep(feat, outs, F32), *pair(4 * feat, outs), plain,
     ]
     whole = pl.BlockSpec(memory_space=pltpu.VMEM)
+    grain = 8 * lax.axis_size(REDUCE_AXES)
     return pl.pallas_call(
         functools.partial(step_kernel, rows),
-        out_shape=jax.ShapeDtypeStruct((15 * feat, wide), F32),
+        out_shape=jax.ShapeDtypeStruct((-(-15 * feat // grain) * grain, wide), F32),
         in_specs=[whole] * 9,
         out_specs=whole,
         scratch_shapes=scratch,
@@ -333,7 +432,7 @@
     inside = ((rows >= 0) & (rows < total_rows)).astype(F32)
     mask = jnp.broadcast_to(inside[:, None], (row_count + 8, real_images.shape[3]))
     packed = local_step(vr, vf, ro, mask, rgb_weight, first_weight, second_weight, skip_weight)
-    return unpack(lax.psum(packed, ("band", "img", "col")), skip_weight.shape[0])
+    return unpack(reduce_all(packed), skip_weight.shape[0])
 
 
 def solution(mesh):

time: 154 us -> 74.4 us (0.48)
  waiting for transfers between devices: 96 us -> 0.7 us
  Pallas kernels: 9.64 us -> 37 us
  between operations: 14.3 us -> 0.86 us
  local copies, waits for them, and re-layouts: 11.1 us -> 12.8 us
    psum x1 -> x0, waiting for transfers between devices: 95.3 us -> none  [body(): lax.psum(packed, ('band', 'img', 'col'))]
    pallas_call x0 -> x1, Pallas kernels: none -> 27.4 us  [reduce_all(): pl.pallas_call(functools.partial(reduce_kernel, sizes), out_shape=jax.Sha...]
    unnamed x18 -> x16, local copies, waits for them, and re-layouts: 3.83 us -> 3.81 us
  transfers between devices with their start and end apart: 7 -> 6, of which waited for: 2 -> 1; matrix products, arithmetic and copies ran while one was open for 4% -> 8% of each run, Pallas kernels for 0% -> 0%
where the time goes in v1:
time: 74.4 us; the launch traced here: 73.7 us
  Pallas kernels  37 us (50%)
  starting transfers between devices  13.1 us (18%)
  local copies, waits for them, and re-layouts  12.8 us (17%)
  blocking collectives  6.52 us (9%)
  other arithmetic  2.8 us (4%)
  between operations  0.86 us (1%)
    pallas_call x1, Pallas kernels, reduce_all(): pl.pallas_call(functools.partial(reduce_kernel, sizes), out_shape=jax.Sha...  27.4 us
    pallas_call x1, Pallas kernels, local_step(): pl.pallas_call(functools.partial(step_kernel, rows), out_shape=jax.ShapeD...  9.65 us
    ppermute x3, starting transfers between devices, neighbours(): before = lax.ppermute(cells[cells.shape[0] - above:], axes, down)  9.2 us
    all_to_all x1, blocking collectives, body(): lax.all_to_all(tile_images, 'col', split_axis=1, concat_axis=3, tiled=True)  6.52 us
    ppermute x3, starting transfers between devices, neighbours(): after = lax.ppermute(cells[:below], axes, up)  3.85 us
    unnamed x16, local copies, waits for them, and re-layouts  3.81 us
    concatenate x3, other arithmetic, neighbours(): return jnp.concatenate([before, cells, after], 0)  2.07 us
    slice x1, local copies, waits for them, and re-layouts, unpack(): second = total[:9 * feat].reshape(3, 3, feat, total.shape[1])  1.73 us
  transfers between devices with their start and end apart: 6, of which 1 were waited for; matrix products, arithmetic and copies ran while one was open for 8% of the time, Pallas kernels for 0%

profile of v1, /device:TPU:0, one launch (start us, length us, event | category | flops | bytes accessed | tf_op | source)
XLA Modules:
  0.0 73.7 jit_solution(10189737220988924440)
XLA Ops:
  0.6 0.7 copy.65
  1.3 0.0 copy-start.2
  1.4 2.4 %collective-permute-start = (f32[4,3,128]{2,1,0:T(4,128)S(1)}, f32[4,3,128]{2,1,0:T(4,128)S(1)}, u32[]{:S(2)}, u32[]{:S(2)}) collective-permute-start(f32[4,3,128]{2,1,0:T(4,128)S(1)} %get-tuple-element.25), channel_id=1, source_target_pairs={{0,1},{1,4},{4,5},{5,8},{8,9},{9,12},{12,13},{2,3},{3,6},{6,7},{7,... | collective-permute-start | bytes 18440 | tf_op jit(solution)/shard_map/ppermute | solution.py:407
  3.8 1.3 %collective-permute-start.1 = (f32[4,3,128]{2,1,0:T(4,128)S(1)}, f32[4,3,128]{2,1,0:T(4,128)S(1)}, u32[]{:S(2)}, u32[]{:S(2)}) collective-permute-start(f32[4,3,128]{2,1,0:T(4,128)S(1)} %get-tuple-element.26), channel_id=1, source_target_pairs={{1,0},{4,1},{5,4},{8,5},{9,8},{12,9},{13,12},{3,2},{6,3},{7,6},{10... | collective-permute-start | bytes 18440 | tf_op jit(solution)/shard_map/ppermute | solution.py:408
  5.1 0.0 copy-done.2
  5.1 0.0 copy-start.1
  5.1 0.1 reshape.41
  5.2 6.5 %all_to_all.15 = f32[2,1,1536]{2,1,0:T(1,128)S(1)} all-to-all(f32[2,1,1536]{2,1,0:T(1,128)S(1)} %reshape.41), channel_id=1, replica_groups=mesh['groups'=2,'band'=4,'img'=2,'col'=2] {'col'}, dimensions={0} | all-to-all | bytes 24576 | tf_op jit(solution)/shard_map/all_to_all | solution.py:427
  11.7 0.5 broadcast.22
  12.2 0.7 reduce
  12.9 0.1 reshape.42
  13.0 0.1 slice.70
  13.1 1.3 %collective-permute-start.3 = (f32[2,3,128]{2,1,0:T(4,128)S(1)}, f32[2,3,128]{2,1,0:T(4,128)S(1)}, u32[]{:S(2)}, u32[]{:S(2)}) collective-permute-start(f32[2,3,128]{2,1,0:T(4,128)S(1)} %copy.46), channel_id=1, source_target_pairs={{1,0},{4,1},{5,4},{8,5},{9,8},{12,9},{13,12},{3,2},{6,3},{7,6},{10... | collective-permute-start | bytes 9224 | tf_op jit(solution)/shard_map/ppermute | solution.py:408
  14.4 0.1 slice.68
  14.5 3.0 %collective-permute-start.2 = (f32[2,3,128]{2,1,0:T(4,128)S(1)}, f32[2,3,128]{2,1,0:T(4,128)S(1)}, u32[]{:S(2)}, u32[]{:S(2)}) collective-permute-start(f32[2,3,128]{2,1,0:T(4,128)S(1)} %copy.45), channel_id=1, source_target_pairs={{0,1},{1,4},{4,5},{5,8},{8,9},{9,12},{12,13},{2,3},{3,6},{6,7},{7,... | collective-permute-start | bytes 9224 | tf_op jit(solution)/shard_map/ppermute | solution.py:407
  17.5 0.0 copy-done.1
  17.6 0.1 copy.48
  17.7 0.0 copy-start
  17.7 3.8 %collective-permute-start.4 = (f32[2,128,64]{2,1,0:T(8,128)S(1)}, f32[2,128,64]{2,1,0:T(8,128)S(1)}, u32[]{:S(2)}, u32[]{:S(2)}) collective-permute-start(f32[2,128,64]{2,1,0:T(8,128)S(1)} %get-tuple-element.19), channel_id=1, source_target_pairs={{0,1},{1,4},{4,5},{5,8},{8,9},{9,12},{12,13},{2,3},{3,6},{6,7},{7,... | collective-permute-start | bytes 196616 | tf_op jit(solution)/shard_map/ppermute | solution.py:407
  21.5 0.0 copy-done
  21.6 0.1 squeeze.7
  21.7 0.0 copy-start.3
  21.7 0.7 copy-done.3
  22.4 0.7 copy.51
  23.0 0.2 copy.53
  23.3 0.9 %reshape.37.wt = f32[192,192]{1,0:T(8,128)} reshape(f32[3,64,3,64]{3,2,1,0:T(4,128)S(1)} %copy.53) | data formatting | bytes 294912 | tf_op jit(solution)/shard_map/reshape | solution.py:362
  24.2 0.2 copy.52
  24.4 0.9 %reshape.36.wf = f32[192,192]{1,0:T(8,128)} reshape(f32[3,64,3,64]{3,2,1,0:T(4,128)S(1)} %copy.52) | data formatting | bytes 294912 | tf_op jit(solution)/shard_map/reshape | solution.py:361
  25.3 0.0 collective-permute-done.3
  25.3 1.3 %collective-permute-start.5 = (f32[2,128,64]{2,1,0:T(8,128)S(1)}, f32[2,128,64]{2,1,0:T(8,128)S(1)}, u32[]{:S(2)}, u32[]{:S(2)}) collective-permute-start(f32[2,128,64]{2,1,0:T(8,128)S(1)} %get-tuple-element.20), channel_id=1, source_target_pairs={{1,0},{4,1},{5,4},{8,5},{9,8},{12,9},{13,12},{3,2},{6,3},{7,6},{10... | collective-permute-start | bytes 196616 | tf_op jit(solution)/shard_map/ppermute | solution.py:408
  26.6 0.0 collective-permute-done.2
  26.6 0.6 pad_maximum_fusion.3.vf
  27.2 0.0 collective-permute-done
  27.2 0.0 collective-permute-done.1
  27.2 0.6 pad_maximum_fusion.2.vr
  27.9 0.0 collective-permute-done.4
  27.9 0.7 collective-permute-done.5
  28.6 0.8 %pad_maximum_fusion.ro = f32[8,128,64]{2,1,0:T(8,128)} fusion(f32[2,128,64]{2,1,0:T(8,128)S(1)} %collective-permute-done.5, f32[4,128,64]{2,1,0:T(8,128)S(1)} %copy.48, f32[2,128,64]{2,1,0:T(8,128)S(1)} %collective-permute-done.4), kind=kLoop, calls=%fused_computation | loop fusion | flops 131072 | bytes 524288 | tf_op jit(solution)/shard_map/concatenate | solution.py:409
  29.4 0.7 broadcast_in_dim.2.mask
  30.1 9.6 %shard_map.102.x = f32[1024,128]{1,0:T(8,128)} custom-call(f32[16,3,128]{2,1,0:T(4,128)} %pad_maximum_fusion.2.vr, f32[12,3,128]{2,1,0:T(4,128)} %pad_maximum_fusion.3.vf, f32[8,128,64]{2,1,0:T(8,128)} %pad_maximum_fusion.ro, f32[16,128]{1,0:T(8,128)} %broadcast_in_dim.2.mask, f32[64,3]{1,0:T(8,128)} %bitcast.51, f32[192,192]{1,0:T(8,128)} %reshape.36.wf, ...), custom_call_target="tpu_custom_call" | custom-call | tf_op jit(solution)/shard_map/pallas_call | solution.py:391
  39.7 27.4 %shard_map.103 = f32[1024,128]{1,0:T(8,128)} custom-call(f32[1024,128]{1,0:T(8,128)} %shard_map.102.x), custom_call_target="tpu_custom_call" | custom-call | tf_op jit(solution)/shard_map/pallas_call | solution.py:347
  67.1 1.4 %slice.81 = f32[64,128]{1,0:T(8,128)} slice(f32[1024,128]{1,0:T(8,128)} %shard_map.103), slice={[576:640], [0:128]} | slice | bytes 65536 | tf_op jit(solution)/shard_map/slice | solution.py:414
  68.5 0.8 %slice_bitcast_fusion.3 = f32[3,64]{0,1:T(8,128)S(1)} fusion(f32[1024,128]{1,0:T(8,128)} %shard_map.103), kind=kLoop, calls=%fused_computation.8 | loop fusion | bytes 1536 | tf_op jit(solution)/shard_map/transpose | solution.py:420
  69.3 0.9 %slice_bitcast_fusion.2 = (f32[1,64,64]{2,1,0:T(8,128)S(1)}, f32[1,64,64]{2,1,0:T(8,128)S(1)}, f32[1,64,64]{2,1,0:T(8,128)S(1)}) fusion(f32[1024,128]{1,0:T(8,128)} %shard_map.103), kind=kLoop, calls=%fused_computation.7 | loop fusion | bytes 98304 | tf_op jit(solution)/shard_map/stack | solution.py:418
  70.2 0.0 slice-start
  70.2 1.7 %slice.80 = f32[576,128]{1,0:T(8,128)} slice(f32[1024,128]{1,0:T(8,128)} %shard_map.103), slice={[0:576], [0:128]} | slice | bytes 589824 | tf_op jit(solution)/shard_map/slice | solution.py:413
  71.9 0.7 copy.56
  72.6 0.0 slice-done
  72.6 0.2 reshape.39
  72.8 0.2 fusion.1
  73.0 0.7 copy.57
  (12 shorter events, 0.1 us)
Async XLA Ops:
  1.3 3.7 %copy-start.2 = (f32[1,16,3,64]{3,1,2,0:T(8,128)S(1)}, f32[1,16,3,64]{3,1,2,0:T(8,128)}, u32[]{:S(2)}) copy-start(f32[1,16,3,64]{3,1,2,0:T(8,128)} %param.8) | copy-start | bytes 36868
  1.4 25.9 %collective-permute-start = (f32[4,3,128]{2,1,0:T(4,128)S(1)}, f32[4,3,128]{2,1,0:T(4,128)S(1)}, u32[]{:S(2)}, u32[]{:S(2)}) collective-permute-start(f32[4,3,128]{2,1,0:T(4,128)S(1)} %get-tuple-element.25), channel_id=1, source_target_pairs={{0,1},{1,4},{4,5},{5,8},{8,9},{9,12},{12,13},{2,3},{3,6},{6,7},{7,... | collective-permute-start | bytes 18440 | tf_op jit(solution)/shard_map/ppermute | solution.py:407
  3.8 23.5 %collective-permute-start.1 = (f32[4,3,128]{2,1,0:T(4,128)S(1)}, f32[4,3,128]{2,1,0:T(4,128)S(1)}, u32[]{:S(2)}, u32[]{:S(2)}) collective-permute-start(f32[4,3,128]{2,1,0:T(4,128)S(1)} %get-tuple-element.26), channel_id=1, source_target_pairs={{1,0},{4,1},{5,4},{8,5},{9,8},{12,9},{13,12},{3,2},{6,3},{7,6},{10... | collective-permute-start | bytes 18440 | tf_op jit(solution)/shard_map/ppermute | solution.py:408
  5.1 12.5 %copy-start.1 = (f32[4,128,64]{1,2,0:T(8,128)S(1)}, f32[4,128,64]{1,2,0:T(8,128)}, u32[]{:S(2)}) copy-start(f32[4,128,64]{1,2,0:T(8,128)} %param.13) | copy-start | bytes 393220
  13.1 12.2 %collective-permute-start.3 = (f32[2,3,128]{2,1,0:T(4,128)S(1)}, f32[2,3,128]{2,1,0:T(4,128)S(1)}, u32[]{:S(2)}, u32[]{:S(2)}) collective-permute-start(f32[2,3,128]{2,1,0:T(4,128)S(1)} %copy.46), channel_id=1, source_target_pairs={{1,0},{4,1},{5,4},{8,5},{9,8},{12,9},{13,12},{3,2},{6,3},{7,6},{10... | collective-permute-start | bytes 9224 | tf_op jit(solution)/shard_map/ppermute | solution.py:408
  14.5 12.1 %collective-permute-start.2 = (f32[2,3,128]{2,1,0:T(4,128)S(1)}, f32[2,3,128]{2,1,0:T(4,128)S(1)}, u32[]{:S(2)}, u32[]{:S(2)}) collective-permute-start(f32[2,3,128]{2,1,0:T(4,128)S(1)} %copy.45), channel_id=1, source_target_pairs={{0,1},{1,4},{4,5},{5,8},{8,9},{9,12},{12,13},{2,3},{3,6},{6,7},{7,... | collective-permute-start | bytes 9224 | tf_op jit(solution)/shard_map/ppermute | solution.py:407
  17.7 3.8 %copy-start = (f32[3,3,64,64]{3,2,1,0:T(8,128)S(1)}, f32[3,3,64,64]{3,2,1,0:T(8,128)}, u32[]{:S(2)}) copy-start(f32[3,3,64,64]{3,2,1,0:T(8,128)} %param.10) | copy-start | bytes 442372
  17.7 10.1 %collective-permute-start.4 = (f32[2,128,64]{2,1,0:T(8,128)S(1)}, f32[2,128,64]{2,1,0:T(8,128)S(1)}, u32[]{:S(2)}, u32[]{:S(2)}) collective-permute-start(f32[2,128,64]{2,1,0:T(8,128)S(1)} %get-tuple-element.19), channel_id=1, source_target_pairs={{0,1},{1,4},{4,5},{5,8},{8,9},{9,12},{12,13},{2,3},{3,6},{6,7},{7,... | collective-permute-start | bytes 196616 | tf_op jit(solution)/shard_map/ppermute | solution.py:407
  21.7 0.7 copy-start.3
  25.3 3.2 %collective-permute-start.5 = (f32[2,128,64]{2,1,0:T(8,128)S(1)}, f32[2,128,64]{2,1,0:T(8,128)S(1)}, u32[]{:S(2)}, u32[]{:S(2)}) collective-permute-start(f32[2,128,64]{2,1,0:T(8,128)S(1)} %get-tuple-element.20), channel_id=1, source_target_pairs={{1,0},{4,1},{5,4},{8,5},{9,8},{12,9},{13,12},{3,2},{6,3},{7,6},{10... | collective-permute-start | bytes 196616 | tf_op jit(solution)/shard_map/ppermute | solution.py:408
  70.2 2.4 %slice-start = ((f32[1024,128]{1,0:T(8,128)}), f32[192,128]{1,0:T(8,128)S(1)}, s32[]{:S(2)}) async-start(f32[1024,128]{1,0:T(8,128)} %shard_map.103), calls=%async_computation.1 | async-start | bytes 196608 | tf_op jit(solution)/shard_map/slice | solution.py:415

commit v2 on v1

--- a/solution.py
+++ b/solution.py
@@ -71,7 +71,7 @@
     picks = [(pick_col == 2 * pick_row + (j - 1)).astype(F32).astype(BF16) for j in range(3)]
     out_rows = rows // 2
     for t in range(out_rows + 4):
-        hi, lo = halves(ro[t] * INV_ROOT)
+        hi, lo = halves(ro[t] * (INV_ROOT * mask[2 * t : 2 * t + 1, :half]))
         uz_h[:, at(t)] = dot_nn(hi, picks[1]).astype(BF16)
         uz_l[:, at(t)] = dot_nn(lo, picks[1]).astype(BF16)
         if 2 <= t < 2 + out_rows:
@@ -104,7 +104,7 @@
         lo_ref[:, at(w)] = lo
 
     for w in range(last + 4):
-        u = project(vr[w])
+        u = project(vr[w] * mask[w : w + 1, :])
         s = sigmoid(u)
         value = u * s
         put(fr_h, fr_l, w, value)
@@ -113,7 +113,7 @@
         sp[:, at(w)] = s * (1.0 + u * (1.0 - s))
         s2[:, at(w)] = s * (1.0 - s) * (2.0 + u * (1.0 - 2.0 * s))
     for w in range(2, last + 2):
-        u = project(vf[w - 2])
+        u = project(vf[w - 2] * mask[w : w + 1, :])
         s = sigmoid(u)
         value = u * s
         put(ff_h, ff_l, w, value)
@@ -398,15 +398,63 @@
     )(vr, vf, ro, mask, rgb_weight.T, wf, wt, w2, skip_weight)
 
 
-def neighbours(cells, above, below):
-    axes = ("band", "col")
-    count = lax.axis_size(axes)
-    links = count - 1
-    down = [(i, i + 1) for i in range(links)]
-    up = [(i + 1, i) for i in range(links)]
-    before = lax.ppermute(cells[cells.shape[0] - above :], axes, down)
-    after = lax.ppermute(cells[:below], axes, up)
-    return jnp.concatenate([before, cells, after], 0)
+def halo_kernel(widths, count, inner, *refs):
+    number = len(widths)
+    fields, wholes = refs[:number], refs[number : 2 * number]
+    sends, arrivals = refs[2 * number], refs[2 * number + 1]
+    position = lax.axis_index("band") * inner + lax.axis_index("col")
+
+    def device(place):
+        return {"band": place // inner, "col": lax.rem(place, inner)}
+
+    after = device(lax.rem(position + 1, count))
+    before = device(lax.rem(position + count - 1, count))
+    barrier = pltpu.get_barrier_semaphore()
+    for peer in (after, before):
+        pl.semaphore_signal(
+            barrier, inc=1, device_id=peer, device_id_type=pl.DeviceIdType.MESH
+        )
+    pl.semaphore_wait(barrier, 2)
+    copies = []
+    for k in range(number):
+        width, size = widths[k], fields[k].shape[0]
+        moves = ((size - width, 0, after), (0, size + width, before))
+        for side, (source, target, peer) in enumerate(moves):
+            copies.append(
+                pltpu.make_async_remote_copy(
+                    src_ref=fields[k].at[pl.ds(source, width)],
+                    dst_ref=wholes[k].at[pl.ds(target, width)],
+                    send_sem=sends.at[2 * k + side],
+                    recv_sem=arrivals.at[2 * k + side],
+                    device_id=peer,
+                    device_id_type=pl.DeviceIdType.MESH,
+                )
+            )
+    for copy in copies:
+        copy.start()
+    for k in range(number):
+        width, size = widths[k], fields[k].shape[0]
+        wholes[k][width : width + size] = fields[k][...]
+    for copy in copies:
+        copy.wait()
+
+
+def neighbours(fields, widths):
+    inner = lax.axis_size("col")
+    count = lax.axis_size("band") * inner
+    whole = pl.BlockSpec(memory_space=pltpu.VMEM)
+    number = len(fields)
+    return pl.pallas_call(
+        functools.partial(halo_kernel, widths, count, inner),
+        out_shape=[
+            jax.ShapeDtypeStruct((x.shape[0] + 2 * w,) + x.shape[1:], F32)
+            for x, w in zip(fields, widths)
+        ],
+        in_specs=[whole] * number,
+        out_specs=[whole] * number,
+        scratch_shapes=[pltpu.SemaphoreType.DMA((2 * number,))] * 2,
+        compiler_params=pltpu.CompilerParams(collective_id=1, has_side_effects=True),
+    )(*fields)
 
 
 def unpack(total, feat):
@@ -425,9 +473,7 @@
     axes = ("band", "col")
     total_rows = row_count * lax.axis_size(axes)
     generated = lax.all_to_all(tile_images, "col", split_axis=1, concat_axis=3, tiled=True)
-    vr = neighbours(real_images[0], 4, 4)
-    vf = neighbours(generated[0], 2, 2)
-    ro = neighbours(readout, 2, 2)
+    vr, vf, ro = neighbours((real_images[0], generated[0], readout), (4, 2, 2))
     rows = lax.axis_index(axes) * row_count - 4 + jnp.arange(row_count + 8)
     inside = ((rows >= 0) & (rows < total_rows)).astype(F32)
     mask = jnp.broadcast_to(inside[:, None], (row_count + 8, real_images.shape[3]))

time: 74.4 us -> 65.3 us (0.88)
  starting transfers between devices: 13.1 us -> 3.23 us
  Pallas kernels: 37 us -> 44.8 us
  blocking collectives: 6.52 us -> 0 us
  local copies, waits for them, and re-layouts: 12.8 us -> 15.1 us
  other arithmetic: 2.8 us -> 0.74 us
    ppermute x6 -> x0, starting transfers between devices: 13.1 us -> none  [the longest x3 9.2 us: neighbours(): before = lax.ppermute(cells[cells.shape[0] - above:], axes, down)]
    pallas_call x0 -> x1, Pallas kernels: none -> 10.7 us  [neighbours(): pl.pallas_call(functools.partial(halo_kernel, widths, count, inner), out_...]
    all_to_all x1 -> x0, blocking collectives: 6.52 us -> none  [body(): lax.all_to_all(tile_images, 'col', split_axis=1, concat_axis=3, tiled=True)]
    all_to_all x0 -> x1, starting transfers between devices: none -> 3.23 us  [body(): lax.all_to_all(tile_images, 'col', split_axis=1, concat_axis=3, tiled=True)]
    pallas_call x1, Pallas kernels: 27.4 us -> 24.4 us  [reduce_all(): pl.pallas_call(functools.partial(reduce_kernel, sizes), out_shape=jax.Sha...]
    concatenate x3 -> x0, other arithmetic: 2.07 us -> none  [neighbours(): return jnp.concatenate([before, cells, after], 0)]
    unnamed x16, local copies, waits for them, and re-layouts: 3.81 us -> 5.77 us
  transfers between devices with their start and end apart: 6 -> 1, of which waited for: 1 -> 0; matrix products, arithmetic and copies ran while one was open for 8% -> 1% of each run, Pallas kernels for 0% -> 0%
where the time goes in v2:
time: 65.3 us; the launch traced here: 64.7 us
  Pallas kernels  44.8 us (69%)
  local copies, waits for them, and re-layouts  15.1 us (23%)
  starting transfers between devices  3.23 us (5%)
  between operations  0.76 us (1%)
  other arithmetic  0.74 us (1%)
    pallas_call x1, Pallas kernels, reduce_all(): pl.pallas_call(functools.partial(reduce_kernel, sizes), out_shape=jax.Sha...  24.4 us
    pallas_call x1, Pallas kernels, neighbours(): pl.pallas_call(functools.partial(halo_kernel, widths, count, inner), out_...  10.7 us
    pallas_call x1, Pallas kernels, local_step(): pl.pallas_call(functools.partial(step_kernel, rows), out_shape=jax.ShapeD...  9.69 us
    unnamed x16, local copies, waits for them, and re-layouts  5.77 us
    all_to_all x1, starting transfers between devices, body(): lax.all_to_all(tile_images, 'col', split_axis=1, concat_axis=3, tiled=True)  3.23 us
    slice x1, local copies, waits for them, and re-layouts, unpack(): second = total[:9 * feat].reshape(3, 3, feat, total.shape[1])  1.73 us
    slice x1, local copies, waits for them, and re-layouts, unpack(): skip = total[9 * feat:10 * feat]  1.38 us
  transfers between devices with their start and end apart: 1, of which 0 were waited for; matrix products, arithmetic and copies ran while one was open for 1% of the time, Pallas kernels for 0%

profile of v2, /device:TPU:0, one launch (start us, length us, event | category | flops | bytes accessed | tf_op | source)
XLA Modules:
  0.0 64.7 jit_solution(7268522519265844404)
XLA Ops:
  0.6 0.8 %copy.49 = f32[1,16,3,64]{3,2,0,1:T(4,128)S(1)} copy(f32[1,16,3,64]{3,1,2,0:T(8,128)} %param.8) | data formatting | bytes 24576 | tf_op args[1]
  1.4 0.7 %reshape.37 = f32[2,1,1536]{2,1,0:T(1,128)} reshape(f32[16,1,3,64]{3,2,1,0:T(4,128)S(1)} %bitcast.42) | data formatting | bytes 24576
  2.1 3.2 %all-to-all-start = ((f32[2,1,1536]{2,1,0:T(1,128)}), f32[2,1,1536]{2,1,0:T(1,128)S(1)}, u32[]{:S(2)}, u32[]{:S(2)}) async-start(f32[2,1,1536]{2,1,0:T(1,128)} %reshape.37), calls=%async_computation | async-start | bytes 24576 | tf_op jit(solution)/shard_map/all_to_all | solution.py:475
  5.3 0.0 copy-start.2
  5.3 0.7 %copy-done.2 = f32[1,8,3,128]{3,1,2,0:T(8,128)S(1)} copy-done((f32[1,8,3,128]{3,1,2,0:T(8,128)S(1)}, f32[1,8,3,128]{3,1,2,0:T(8,128)}, u32[]{:S(2)}) %copy-start.2) | copy-done | bytes 12312
  6.0 0.0 copy-start.1
  6.0 0.6 copy.48
  6.6 0.0 all-to-all-done
  6.7 0.5 broadcast.22
  7.2 0.0 copy-start.3
  7.2 0.7 %reduce = f32[2,1536]{1,0:T(2,128)S(1)} reduce(f32[2,1,1536]{2,1,0:T(1,128)S(1)} %all-to-all-done, f32[]{:T(128)} %broadcast.22), dimensions={1}, to_apply=%all_to_all.11.reduce_sub_computation | reduce | bytes 24580 | tf_op jit(solution)/shard_map/all_to_all | solution.py:475
  7.9 0.0 copy-start
  7.9 0.1 reshape.38
  8.0 0.1 squeeze.7
  8.1 0.6 copy.33.refs_1_
  8.7 0.0 copy-done.3
  8.7 0.7 %copy.35 = f32[3,64]{0,1:T(8,128)} copy(f32[3,64]{1,0:T(4,128)S(1)} %copy-done.3) | data formatting | bytes 1536 | tf_op args[2]
  9.4 0.0 copy-done.1
  9.4 0.8 %copy.34.refs_2_ = f32[4,128,64]{2,1,0:T(8,128)} copy(f32[4,128,64]{1,2,0:T(8,128)S(1)} %copy-done.1) | data formatting | bytes 262144 | tf_op args[6]
  10.3 0.0 copy-done
  10.3 0.2 copy.37
  10.5 0.9 %reshape.33.wt = f32[192,192]{1,0:T(8,128)} reshape(f32[3,64,3,64]{3,2,1,0:T(4,128)S(1)} %copy.37) | data formatting | bytes 294912 | tf_op jit(solution)/shard_map/reshape | solution.py:362
  11.4 0.2 copy.36
  11.6 0.9 %reshape.32.wf = f32[192,192]{1,0:T(8,128)} reshape(f32[3,64,3,64]{3,2,1,0:T(4,128)S(1)} %copy.36) | data formatting | bytes 294912 | tf_op jit(solution)/shard_map/reshape | solution.py:361
  12.6 10.7 %shard_map.102 = (f32[16,3,128]{2,1,0:T(4,128)}, f32[12,3,128]{2,1,0:T(4,128)}, f32[8,128,64]{2,1,0:T(8,128)}) custom-call(f32[8,3,128]{2,1,0:T(4,128)} %bitcast.44, f32[8,3,128]{2,1,0:T(4,128)} %copy.33.refs_1_, f32[4,128,64]{2,1,0:T(8,128)} %copy.34.refs_2_), custom_call_target="tpu_custom_call" | custom-call | tf_op jit(solution)/shard_map/pallas_call | solution.py:447
  23.2 0.7 %broadcast_in_dim.2.mask = f32[16,128]{1,0:T(8,128)} broadcast(f32[16]{0:T(128)S(1)} %and_convert_fusion), dimensions={0} | broadcast | bytes 8256 | tf_op jit(solution)/shard_map/broadcast_in_dim | solution.py:479
  23.9 9.7 %shard_map.103.x = f32[1024,128]{1,0:T(8,128)} custom-call(f32[16,3,128]{2,1,0:T(4,128)} %get-tuple-element.7.vr, f32[12,3,128]{2,1,0:T(4,128)} %get-tuple-element.8.vf, f32[8,128,64]{2,1,0:T(8,128)} %get-tuple-element.9.ro, f32[16,128]{1,0:T(8,128)} %broadcast_in_dim.2.mask, f32[64,3]{1,0:T(8,128)} %bitcast.40, f32[192,192]{1,0:T(8,128)} %reshape.32.wf, ...), custom_call_target="tpu_custom_call" | custom-call | tf_op jit(solution)/shard_map/pallas_call | solution.py:391
  33.6 24.4 %shard_map.104 = f32[1024,128]{1,0:T(8,128)} custom-call(f32[1024,128]{1,0:T(8,128)} %shard_map.103.x), custom_call_target="tpu_custom_call" | custom-call | tf_op jit(solution)/shard_map/pallas_call | solution.py:347
  58.0 1.4 %slice.41 = f32[64,128]{1,0:T(8,128)} slice(f32[1024,128]{1,0:T(8,128)} %shard_map.104), slice={[576:640], [0:128]} | slice | bytes 65536 | tf_op jit(solution)/shard_map/slice | solution.py:462
  59.4 0.8 %slice_bitcast_fusion.3 = f32[3,64]{0,1:T(8,128)S(1)} fusion(f32[1024,128]{1,0:T(8,128)} %shard_map.104), kind=kLoop, calls=%fused_computation.6 | loop fusion | bytes 1536 | tf_op jit(solution)/shard_map/transpose | solution.py:468
  60.2 0.9 %slice_bitcast_fusion.2 = (f32[1,64,64]{2,1,0:T(8,128)S(1)}, f32[1,64,64]{2,1,0:T(8,128)S(1)}, f32[1,64,64]{2,1,0:T(8,128)S(1)}) fusion(f32[1024,128]{1,0:T(8,128)} %shard_map.104), kind=kLoop, calls=%fused_computation.5 | loop fusion | bytes 98304 | tf_op jit(solution)/shard_map/stack | solution.py:466
  61.2 0.0 slice-start
  61.2 1.7 %slice.40 = f32[576,128]{1,0:T(8,128)} slice(f32[1024,128]{1,0:T(8,128)} %shard_map.104), slice={[0:576], [0:128]} | slice | bytes 589824 | tf_op jit(solution)/shard_map/slice | solution.py:461
  62.9 0.7 %copy.40 = f32[3,64]{1,0:T(4,128)} copy(f32[3,64]{0,1:T(8,128)S(1)} %slice_bitcast_fusion.3) | data formatting | bytes 1536
  63.5 0.0 slice-done
  63.5 0.2 reshape.35
  63.7 0.2 fusion
  63.9 0.7 %copy.41 = f32[3,3,64,64]{3,2,1,0:T(8,128)} copy(f32[3,3,64,64]{3,2,0,1:T(8,128)S(1)} %pad_maximum_fusion) | data formatting | bytes 294912
  (5 shorter events, 0.1 us)
Async XLA Ops:
  2.1 4.6 %all-to-all-start = ((f32[2,1,1536]{2,1,0:T(1,128)}), f32[2,1,1536]{2,1,0:T(1,128)S(1)}, u32[]{:S(2)}, u32[]{:S(2)}) async-start(f32[2,1,1536]{2,1,0:T(1,128)} %reshape.37), calls=%async_computation | async-start | bytes 24576 | tf_op jit(solution)/shard_map/all_to_all | solution.py:475
  5.3 0.7 %copy-start.2 = (f32[1,8,3,128]{3,1,2,0:T(8,128)S(1)}, f32[1,8,3,128]{3,1,2,0:T(8,128)}, u32[]{:S(2)}) copy-start(f32[1,8,3,128]{3,1,2,0:T(8,128)} %param.7) | copy-start | bytes 36868
  6.0 3.4 %copy-start.1 = (f32[4,128,64]{1,2,0:T(8,128)S(1)}, f32[4,128,64]{1,2,0:T(8,128)}, u32[]{:S(2)}) copy-start(f32[4,128,64]{1,2,0:T(8,128)} %param.13) | copy-start | bytes 393220
  7.2 1.5 %copy-start.3 = (f32[3,64]{1,0:T(4,128)S(1)}, f32[3,64]{1,0:T(4,128)}, u32[]{:S(2)}) copy-start(f32[3,64]{1,0:T(4,128)} %param.9) | copy-start | bytes 2308
  7.9 2.4 %copy-start = (f32[3,3,64,64]{3,2,1,0:T(8,128)S(1)}, f32[3,3,64,64]{3,2,1,0:T(8,128)}, u32[]{:S(2)}) copy-start(f32[3,3,64,64]{3,2,1,0:T(8,128)} %param.10) | copy-start | bytes 442372
  61.2 2.4 %slice-start = ((f32[1024,128]{1,0:T(8,128)}), f32[192,128]{1,0:T(8,128)S(1)}, s32[]{:S(2)}) async-start(f32[1024,128]{1,0:T(8,128)} %shard_map.104), calls=%async_computation.1 | async-start | bytes 196608 | tf_op jit(solution)/shard_map/slice | solution.py:463
